TPU v7x, 32 devices: a whole 2x2x4 slice. The times are simulated.
32 devices in a mesh: dp: 8 (over z, x), ctx: 4 (over y, core).
Axes of the slice: x: 2, y: 2, z: 4, core: 2. Of those that a mesh axis runs over, the one named last changes fastest.
Arguments:
- features: bfloat16 [4096, 4096], P(('dp', 'ctx')), may hold values from -6 to 6
- gate_in: bfloat16 [4096, 4096], P(('dp', 'ctx')), may hold values from -6 to 6
- gate_out: bfloat16 [4096, 4096], P(('dp', 'ctx')), may hold values from -6 to 6
- value_weight: bfloat16 [4096, 4096], P('dp', 'ctx'), may hold values from -0.09375 to 0.09375
- short_taps: float32 [3, 7, 4096], replicated, may hold values from -2 to 2
- medium_taps: bfloat16 [128, 256], replicated, may hold values from -0.5 to 0.5
- cotangent: bfloat16 [4096, 4096], P(('dp', 'ctx')), may hold values from -6 to 6
Outputs:
- layer_out: bfloat16 [4096, 4096], P(('dp', 'ctx'))
- grad_features: bfloat16 [4096, 4096], P(('dp', 'ctx'))
- grad_gate_in: bfloat16 [4096, 4096], P(('dp', 'ctx'))
- grad_gate_out: bfloat16 [4096, 4096], P(('dp', 'ctx'))
- grad_weight: bfloat16 [4096, 4096], P('dp', 'ctx')
- grad_short: float32 [3, 7, 4096], P(None, None, 'ctx')
- grad_medium: float32 [128, 256], P(None, 'ctx')
All inputs are finite; a program needn't handle non-finite values.
Results may differ from a plain program's by a relative error of at most 0.025.
Values may be sent and summed in bfloat16 or wider, within the bound.
A program may use at most 256 MiB of HBM per device.

v0:
```python
import math
import jax
import jax.numpy as jnp
from jax import lax
from jax.sharding import PartitionSpec as P


def causal_conv(stream, conv_taps, prior_rows):
    conv_edge = conv_taps.shape[0] - 1
    row_count = stream.shape[0]
    extended = jnp.concatenate([prior_rows, stream], axis=0)
    running = conv_taps[0] * extended[conv_edge : conv_edge + row_count]
    for shift_back in range(1, conv_edge + 1):
        running = (
            running
            + conv_taps[shift_back]
            * extended[conv_edge - shift_back : conv_edge - shift_back + row_count]
        )
    return running


def conv_back(gradient, conv_taps, later_rows):
    conv_edge = conv_taps.shape[0] - 1
    row_count = gradient.shape[0]
    extended = jnp.concatenate([gradient, later_rows], axis=0)
    running = conv_taps[0] * extended[:row_count]
    for ahead in range(1, conv_edge + 1):
        running = running + conv_taps[ahead] * extended[ahead : ahead + row_count]
    return running


def conv_taps_grad(gradient, stream, prior_rows):
    conv_edge = prior_rows.shape[0]
    row_count = stream.shape[0]
    extended = jnp.concatenate([prior_rows, stream], axis=0)
    return jnp.stack(
        [
            jnp.sum(
                gradient * extended[conv_edge - shift_back : conv_edge - shift_back + row_count],
                axis=0,
            )
            for shift_back in range(conv_edge + 1)
        ]
    )


def toeplitz_table(medium):
    filter_span, group_count = medium.shape
    padded = jnp.concatenate(
        [
            jnp.zeros((1, group_count), medium.dtype),
            medium[::-1],
            jnp.zeros((filter_span, group_count), medium.dtype),
        ],
        axis=0,
    )
    tiled = jnp.tile(padded.T, (1, filter_span))
    return tiled[:, : 2 * filter_span * filter_span].reshape(
        group_count, filter_span, 2 * filter_span
    )


def fold_table(grad_table):
    group_count, filter_span, double_span = grad_table.shape
    flat = grad_table.reshape(group_count, filter_span * double_span)
    flat = jnp.concatenate([flat, jnp.zeros((group_count, filter_span), grad_table.dtype)], axis=1)
    summed = jnp.sum(flat.reshape(group_count, filter_span, double_span + 1), axis=1)
    return summed[:, 1 : filter_span + 1][:, ::-1].T


def apply_toeplitz(toeplitz, before, product):
    group_count, filter_span = (toeplitz.shape[0], toeplitz.shape[1])
    row_count, channels = product.shape
    block_shape = (row_count // filter_span, filter_span, group_count, channels // group_count)
    extended = jnp.concatenate([before, product], axis=0)
    lower_half = extended[:row_count].reshape(block_shape)
    upper_half = extended[filter_span:].reshape(block_shape)
    window = jnp.concatenate([lower_half, upper_half], axis=1)
    filtered = jnp.einsum("gij,bjgs->bigs", toeplitz, window, preferred_element_type=jnp.float32)
    return (filtered.reshape(row_count, channels), window)


def toeplitz_back(toeplitz, grad_filtered, later_rows, window):
    group_count, filter_span = (toeplitz.shape[0], toeplitz.shape[1])
    row_count, channels = grad_filtered.shape
    block_shape = (row_count // filter_span, filter_span, group_count, channels // group_count)
    current = grad_filtered.reshape(block_shape)
    following = jnp.concatenate([grad_filtered[filter_span:], later_rows], axis=0).reshape(
        block_shape
    )
    grad_product = jnp.einsum(
        "gij,bigs->bjgs", toeplitz[:, :, filter_span:], current, preferred_element_type=jnp.float32
    )
    grad_product = grad_product + jnp.einsum(
        "gij,bigs->bjgs",
        toeplitz[:, :, :filter_span],
        following,
        preferred_element_type=jnp.float32,
    )
    grad_table = jnp.einsum("bigs,bjgs->gij", current, window, preferred_element_type=jnp.float32)
    return (grad_product.reshape(row_count, channels), fold_table(grad_table))


def mixer_pass(
    stream_in,
    stream_out,
    stream_values,
    cot_rows,
    conv_taps,
    medium,
    fetch_rims,
    fetch_before,
    fetch_after,
    fetch_later,
):
    row_count = stream_in.shape[0]
    filter_span = medium.shape[0]
    conv_edge = conv_taps.shape[1] - 1
    streams = (stream_in, stream_out, stream_values)
    rims = fetch_rims(tuple((stream[row_count - conv_edge :] for stream in streams)))
    convs = [causal_conv(streams[index], conv_taps[index], rims[index]) for index in range(3)]
    product = (convs[0] * convs[2]).astype(jnp.bfloat16)
    toeplitz = toeplitz_table(medium)
    filtered, window = apply_toeplitz(
        toeplitz, fetch_before(product[row_count - filter_span :]), product
    )
    layer_out = (convs[1] * filtered).astype(jnp.bfloat16)
    grad_filtered = (cot_rows * convs[1]).astype(jnp.bfloat16)
    grad_product, medium_grad = toeplitz_back(
        toeplitz, grad_filtered, fetch_after(grad_filtered[:filter_span]), window
    )
    grad_convs = (grad_product * convs[2], cot_rows * filtered, grad_product * convs[0])
    later = fetch_later(tuple((gradient[:conv_edge] for gradient in grad_convs)))
    grad_streams = [
        conv_back(grad_convs[index], conv_taps[index], later[index]) for index in range(3)
    ]
    short_grad = jnp.stack(
        [conv_taps_grad(grad_convs[index], streams[index], rims[index]) for index in range(3)]
    )
    return (layer_out, grad_streams, short_grad, medium_grad)


def zero_tuple(tail_rows):
    return tuple((jnp.zeros_like(piece) for piece in tail_rows))


def local(features, gate_in, gate_out, value_weight, short_taps, medium_taps, cotangent):
    ctx_count = lax.axis_size("ctx")
    dp_count = lax.axis_size("dp")
    ctx_index = lax.axis_index("ctx")
    own_rows, channels = features.shape
    block_cols = value_weight.shape[1]
    group_count = medium_taps.shape[1]
    total_rows = own_rows * ctx_count * dp_count
    row_scale = 1.0 / math.sqrt(total_rows)
    group_scale = 1.0 / math.sqrt(total_rows * (channels // group_count))
    weight_block = lax.all_gather(value_weight, "dp", axis=0, tiled=True)
    feature_window = lax.all_gather(features, "ctx", axis=0, tiled=True)
    values_block = jnp.dot(feature_window, weight_block, preferred_element_type=jnp.float32).astype(
        jnp.bfloat16
    )
    block_in, block_out, block_cot = (
        lax.all_to_all(gate_in, "ctx", split_axis=1, concat_axis=0, tiled=True),
        lax.all_to_all(gate_out, "ctx", split_axis=1, concat_axis=0, tiled=True),
        lax.all_to_all(cotangent, "ctx", split_axis=1, concat_axis=0, tiled=True),
    )
    taps_block = lax.dynamic_slice_in_dim(short_taps, ctx_index * block_cols, block_cols, 2)
    group_block = group_count // ctx_count
    medium_block = lax.dynamic_slice_in_dim(medium_taps, ctx_index * group_block, group_block, 1)
    out_block, grad_streams, short_grad, medium_grad = mixer_pass(
        block_in,
        block_out,
        values_block,
        block_cot,
        taps_block,
        medium_block,
        zero_tuple,
        jnp.zeros_like,
        jnp.zeros_like,
        zero_tuple,
    )
    layer_out = lax.all_to_all(out_block, "ctx", split_axis=0, concat_axis=1, tiled=True)
    grad_gate_in, grad_gate_out = (
        lax.all_to_all(
            grad_streams[0].astype(jnp.bfloat16), "ctx", split_axis=0, concat_axis=1, tiled=True
        ),
        lax.all_to_all(
            grad_streams[1].astype(jnp.bfloat16), "ctx", split_axis=0, concat_axis=1, tiled=True
        ),
    )
    grad_values = grad_streams[2].astype(jnp.bfloat16)
    grad_short, grad_medium = (
        lax.psum((short_grad * row_scale).astype(jnp.bfloat16), "dp").astype(jnp.float32),
        lax.psum((medium_grad * group_scale).astype(jnp.bfloat16), "dp").astype(jnp.float32),
    )
    grad_weight = lax.psum_scatter(
        (
            lax.dot_general(
                feature_window,
                grad_values,
                (((0,), (0,)), ((), ())),
                preferred_element_type=jnp.float32,
            )
            * row_scale
        ).astype(jnp.bfloat16),
        "dp",
        scatter_dimension=0,
        tiled=True,
    )
    grad_features = lax.psum_scatter(
        lax.dot_general(
            grad_values, weight_block, (((1,), (1,)), ((), ())), preferred_element_type=jnp.float32
        ).astype(jnp.bfloat16),
        "ctx",
        scatter_dimension=0,
        tiled=True,
    )
    return (
        layer_out,
        grad_features,
        grad_gate_in,
        grad_gate_out,
        grad_weight,
        grad_short,
        grad_medium,
    )


def solution(mesh):
    in_specs = (
        P(("dp", "ctx"), None),
        P(("dp", "ctx"), None),
        P(("dp", "ctx"), None),
        P("dp", "ctx"),
        P(),
        P(),
        P(("dp", "ctx"), None),
    )
    out_specs = (
        P(("dp", "ctx"), None),
        P(("dp", "ctx"), None),
        P(("dp", "ctx"), None),
        P(("dp", "ctx"), None),
        P("dp", "ctx"),
        P(None, None, "ctx"),
        P(None, "ctx"),
    )
    return jax.shard_map(local, mesh=mesh, in_specs=in_specs, out_specs=out_specs, check_vma=False)
```

profile of v0, /device:TPU:0, one launch (start us, length us, event | category | flops | bytes accessed | tf_op | source)
XLA Modules:
  0.0 425.9 jit_solution(8969090850510553351)
XLA Ops:
  10.0 4.2 all-to-all-start
  15.5 19.7 %all-to-all-done = bf16[128,4,1024]{0,2,1:T(8,128)(2,1)S(1)} async-done(((bf16[128,4,1024]{0,2,1:T(8,128)(2,1)}), bf16[128,4,1024]{0,2,1:T(8,128)(2,1)S(1)}, u32[]{:S(2)}, u32[]{:S(2)}) %all-to-all-start) | async-done | bytes 1048608 | tf_op jit(solution)/shard_map/all_to_all | solution.py:164
  35.3 3.5 all-to-all-start.3
  39.3 3.2 tile.4
  42.5 10.9 %tile.10 = bf16[64,32896]{1,0:T(8,128)(2,1)} reshape(bf16[64,128,257]{2,1,0:T(8,128)(2,1)} %tile.4) | data formatting | bytes 8421376 | tf_op jit(solution)/shard_map/tile | solution.py:57
  55.5 3.1 copy.80
  62.6 3.5 all-to-all-start.1
  70.8 6.7 %fusion.43 = (bf16[512,1024]{1,0:T(8,128)(2,1)S(1)}, f32[512,1024]{1,0:T(8,128)}) fusion(f32[4,128,1024]{2,1,0:T(8,128)S(1)} %copy.56, f32[1024]{0:T(1024)S(1)} %bitcast.192, f32[1024]{0:T(1024)S(1)} %bitcast.194, f32[1024]{0:T(1024)S(1)} %bitcast.196, f32[1024]{0:T(1024)S(1)} %bitcast.198, f32[1024]{0:T(1024)S(1)} %bitcast.200, ...), kind=kLoop, calls=%fused_computation.91 | loop fusion | flops 11534336 | bytes 6320128 | tf_op jit(solution)/shard_map/convert_element_type | solution.py:128
  78.5 2.3 copy.57
  82.9 2.7 fusion.41
  91.3 97.8 %all-gather.5.cloned.1.call-done = bf16[4096,1024]{1,0:T(8,128)(2,1)} async-done(((bf16[512,1024]{1,0:T(8,128)(2,1)}), bf16[4096,1024]{1,0:T(8,128)(2,1)}) %all-gather.5.cloned.1.call-update) | async-done | bytes 8388624 | tf_op jit(solution)/shard_map/all_gather | solution.py:157
  189.1 10.1 %convolution_convert_fusion.1 = bf16[512,1024]{1,0:T(8,128)(2,1)} fusion(bf16[512,4096]{1,0:T(8,128)(2,1)} %all-gather.3.cloned.1.call-done, bf16[4096,1024]{1,0:T(8,128)(2,1)} %all-gather.5.cloned.1.call-done), kind=kOutput, calls=%fused_computation.102 | convolution fusion | flops 4295491584 | bytes 13631488 | tf_op jit(solution)/shard_map/dot_general | solution.py:159
  199.3 8.8 %fusion.27 = (f32[1024]{0:T(1024)S(1)}, f32[1024]{0:T(1024)S(1)}, f32[1024]{0:T(1024)S(1)}, f32[1024]{0:T(1024)S(1)}, f32[1024]{0:T(1024)S(1)}, /*index=5*/f32[1...) fusion(bf16[512,1024]{1,0:T(8,128)(2,1)S(1)} %bitcast.157, ...), kind=kLoop, calls=%fused_computation.69 | loop fusion | flops 22012928 | bytes 9494528 | tf_op jit(solution)/shard_map/reduce_sum | solution.py:38
  208.1 6.7 %fusion.40 = (f32[1024]{0:T(1024)S(1)}, f32[1024]{0:T(1024)S(1)}, f32[1024]{0:T(1024)S(1)}, f32[1024]{0:T(1024)S(1)}, f32[1024]{0:T(1024)S(1)}, /*index=5*/f32[1...) fusion(bf16[512,1024]{1,0:T(8,128)(2,1)S(1)} %copy-done.17, ...), kind=kLoop, calls=%fused_computation.82 | loop fusion | flops 29352960 | bytes 11591680 | tf_op jit(solution)/shard_map/reduce_sum | solution.py:38
  216.6 6.8 %fusion = bf16[4096,1024]{0,1:T(8,128)(2,1)} fusion(bf16[512,1024]{1,0:T(8,128)(2,1)S(1)} %add_convert_fusion.2, bf16[512,4096]{1,0:T(8,128)(2,1)S(1)} %copy-done.21), kind=kOutput, calls=%fused_computation.1 | convolution fusion | flops 4303355904 | bytes 13631488 | tf_op jit(solution)/shard_map/dot_general | solution.py:198
  223.5 9.5 %convolution_convert_fusion = bf16[512,4096]{1,0:T(8,128)(2,1)} fusion(bf16[512,1024]{1,0:T(8,128)(2,1)S(1)} %add_convert_fusion.2, bf16[4096,1024]{1,0:T(8,128)(2,1)} %all-gather.5.cloned.1.call-done), kind=kOutput, calls=%fused_computation.2 | convolution fusion | flops 4297064448 | bytes 13631488 | tf_op jit(solution)/shard_map/dot_general | solution.py:211
  239.5 2.2 reshape.116
  249.4 3.1 copy.53
  252.5 4.6 %fusion.14 = (f32[1024]{0:T(1024)S(1)}, f32[1024]{0:T(1024)S(1)}, f32[1024]{0:T(1024)S(1)}, f32[1024]{0:T(1024)S(1)}, f32[1024]{0:T(1024)S(1)}, /*index=5*/f32[1...) fusion(bf16[512,1024]{1,0:T(8,128)(2,1)S(1)} %bitcast.160, f32[512,1024]{1,0:T(8,128)} %copy.53, ...), kind=kLoop, calls=%fused_computation.56 | loop fusion | flops 11003904 | bytes 10510336 | tf_op jit(solution)/shard_map/reduce_sum | solution.py:38
  257.1 17.6 %all_to_all.108 = bf16[4,128,1024]{2,1,0:T(8,128)(2,1)} all-to-all(bf16[4,128,1024]{2,1,0:T(8,128)(2,1)S(1)} %bitcast.167), channel_id=1, replica_groups=mesh['dp'=8,'ctx'=4] {'ctx'}, dimensions={0} | all-to-all | bytes 2097152 | tf_op jit(solution)/shard_map/all_to_all | solution.py:182
  274.7 4.3 all-to-all-start.4
  279.0 8.3 %add_convert_fusion = bf16[512,1024]{1,0:T(8,128)(2,1)} fusion(f32[512,1024]{1,0:T(8,128)} %get-tuple-element.52, f32[1024]{0:T(1024)S(1)} %bitcast.193, f32[1024]{0:T(1024)S(1)} %bitcast.195, f32[1024]{0:T(1024)S(1)} %bitcast.197, f32[1024]{0:T(1024)S(1)} %bitcast.199, f32[1024]{0:T(1024)S(1)} %bitcast.201, f32[1024]{0:T(1024)S(1)} %bitcast.203, ...), kind=kLoop, calls=%fused_computation.95 | loop fusion | flops 7340032 | bytes 3174400 | tf_op jit(solution)/shard_map/convert_element_type | solution.py:188
  287.3 6.1 %all-to-all-done.4 = bf16[4,128,1024]{2,1,0:T(8,128)(2,1)} async-done(((bf16[4,128,1024]{2,1,0:T(8,128)(2,1)}), bf16[4,128,1024]{2,1,0:T(8,128)(2,1)}, u32[]{:S(2)}, u32[]{:S(2)}) %all-to-all-start.4) | async-done | bytes 1048608 | tf_op jit(solution)/shard_map/all_to_all | solution.py:184
  293.4 4.5 %all-to-all-start.5 = ((bf16[4,128,1024]{2,1,0:T(8,128)(2,1)}), bf16[4,128,1024]{2,1,0:T(8,128)(2,1)}, u32[]{:S(2)}, u32[]{:S(2)}) async-start(bf16[4,128,1024]{2,1,0:T(8,128)(2,1)} %bitcast.170), calls=%async_computation.6 | async-start | bytes 2097152 | tf_op jit(solution)/shard_map/all_to_all | solution.py:187
  299.2 4.7 %copy.84 = f32[8,8,128,256]{3,1,2,0:T(8,128)S(1)} copy(f32[8,8,128,256]{3,2,1,0:T(8,128)S(1)} %bitcast.155) | data formatting | bytes 16777216
  304.0 3.9 concatenate.46
  307.9 14.3 %reshape.123 = f32[64,128,257]{2,1,0:T(8,128)} reshape(f32[64,32896]{1,0:T(8,128)} %concatenate.46) | data formatting | bytes 16842752 | tf_op jit(solution)/shard_map/reshape | solution.py:67
  322.2 6.3 %reduce_sum.219 = f32[64,257]{1,0:T(8,128)S(1)} reduce(f32[64,128,257]{2,1,0:T(8,128)} %reshape.123, f32[]{:T(128)} %constant.1.clone.1), dimensions={1}, to_apply=%region_24.0 | reduce | flops 2088896 | bytes 8487172 | tf_op jit(solution)/shard_map/reduce_sum | solution.py:67
  328.9 36.9 %all-reduce.9 = (bf16[3,7,1024]{2,1,0:T(8,128)(2,1)S(1)}, bf16[128,64]{0,1:T(8,128)(2,1)S(1)}) all-reduce(bf16[3,7,1024]{2,1,0:T(8,128)(2,1)S(1)} %fusion.52, bf16[128,64]{0,1:T(8,128)(2,1)S(1)} %fusion.53), channel_id=1, replica_groups=mesh['dp'=8,'ctx'=4] {'dp'}, use_global_device_ids=true, to_apply=%region_23.0 | all-reduce | flops 29696 | bytes 118784 | tf_op jit(solution)/shard_map/psum | solution.py:193
  369.0 2.3 copy.79
  374.3 2.3 copy.72
  376.6 42.6 %reduce-scatter.3.cloned.1.call-done = bf16[128,4096]{1,0:T(8,128)(2,1)} async-done(((bf16[512,4096]{1,0:T(8,128)(2,1)}), bf16[128,4096]{1,0:T(8,128)(2,1)}) %reduce-scatter.3.cloned.1.call-update) | async-done | bytes 1048592 | tf_op jit(solution)/shard_map/reduce_scatter | solution.py:210
  (108 shorter events, 48.0 us)
Async XLA Ops:
  7.2 31.6 %copy-start = (bf16[128,256]{1,0:T(8,128)(2,1)S(1)}, bf16[128,256]{1,0:T(8,128)(2,1)}, u32[]{:S(2)}) copy-start(bf16[128,256]{1,0:T(8,128)(2,1)} %param.12) | copy-start | bytes 196612
  7.2 1.5 copy-start.18
  7.2 84.1 %all-gather.3.cloned.1.call-start = ((), (), s32[]{:S(2)}) async-start(), calls=%async_computation.8 | async-start | bytes 5242880 | tf_op jit(solution)/shard_map/all_gather | solution.py:158
  7.9 181.2 %all-gather.5.cloned.1.call-start = ((), (), s32[]{:S(2)}) async-start(), calls=%async_computation.9 | async-start | bytes 9437184 | tf_op jit(solution)/shard_map/all_gather | solution.py:157
  8.7 5.6 %copy-start.19 = (bf16[128,4096]{1,0:T(8,128)(2,1)S(1)}, bf16[128,4096]{1,0:T(8,128)(2,1)}, u32[]{:S(2)}) copy-start(bf16[128,4096]{1,0:T(8,128)(2,1)} %param.13) | copy-start | bytes 3145732
  10.0 25.3 %all-to-all-start = ((bf16[128,4,1024]{0,2,1:T(8,128)(2,1)}), bf16[128,4,1024]{0,2,1:T(8,128)(2,1)S(1)}, u32[]{:S(2)}, u32[]{:S(2)}) async-start(bf16[128,4,1024]{0,2,1:T(8,128)(2,1)} %bitcast.1), calls=%async_computation | async-start | bytes 2097152 | tf_op jit(solution)/shard_map/all_to_all | solution.py:164
  35.3 26.0 %copy-start.11 = (bf16[128,4,1024]{0,2,1:T(8,128)(2,1)}, bf16[128,4,1024]{0,2,1:T(8,128)(2,1)S(1)}, u32[]{:S(2)}) copy-start(bf16[128,4,1024]{0,2,1:T(8,128)(2,1)S(1)} %all-to-all-done) | copy-start | bytes 3145732
  35.3 27.4 %all-to-all-start.3 = ((bf16[128,4,1024]{0,2,1:T(8,128)(2,1)}), bf16[128,4,1024]{0,2,1:T(8,128)(2,1)S(1)}, u32[]{:S(2)}, u32[]{:S(2)}) async-start(bf16[128,4,1024]{0,2,1:T(8,128)(2,1)} %bitcast.33), calls=%async_computation.3 | async-start | bytes 2097152 | tf_op jit(solution)/shard_map/all_to_all | solution.py:165
  53.3 2.2 slice-start
  55.5 3.1 copy-start.20
  62.6 136.6 %all-to-all-start.1 = ((bf16[128,4,1024]{2,0,1:T(8,128)(2,1)}), bf16[128,4,1024]{2,0,1:T(8,128)(2,1)S(1)}, u32[]{:S(2)}, u32[]{:S(2)}) async-start(bf16[128,4,1024]{2,0,1:T(8,128)(2,1)} %bitcast.169), calls=%async_computation.1 | async-start | bytes 2097152 | tf_op jit(solution)/shard_map/all_to_all | solution.py:163
  66.2 308.1 %reduce-scatter.5.cloned.1.call-start = ((), (), s32[]{:S(2)}) async-start(), calls=%async_computation.11 | async-start | bytes 9437184 | tf_op jit(solution)/shard_map/reduce_scatter | solution.py:196
  70.8 6.7 %copy-start.4 = (f32[4,128,1024]{2,1,0:T(8,128)}, f32[4,128,1024]{2,1,0:T(8,128)S(1)}, u32[]{:S(2)}) copy-start(f32[4,128,1024]{2,1,0:T(8,128)S(1)} %copy.56) | copy-start | bytes 6291460
  77.5 1.0 copy-start.15
  82.9 2.7 copy-start.9
  82.9 3.2 copy-start.2
  199.3 8.8 %copy-start.17 = (bf16[512,1024]{1,0:T(8,128)(2,1)S(1)}, bf16[512,1024]{1,0:T(8,128)(2,1)}, u32[]{:S(2)}) copy-start(bf16[512,1024]{1,0:T(8,128)(2,1)} %convolution_convert_fusion.1) | copy-start | bytes 3145732
  208.1 8.5 %copy-start.21 = (bf16[512,4096]{1,0:T(8,128)(2,1)S(1)}, bf16[512,4096]{1,0:T(8,128)(2,1)}, u32[]{:S(2)}) copy-start(bf16[512,4096]{1,0:T(8,128)(2,1)} %all-gather.3.cloned.1.call-done) | copy-start | bytes 12582916
  223.4 195.7 %reduce-scatter.3.cloned.1.call-start = ((), (), s32[]{:S(2)}) async-start(), calls=%async_computation.10 | async-start | bytes 5242880 | tf_op jit(solution)/shard_map/reduce_scatter | solution.py:210
  232.9 1.6 copy-start.13
  238.4 6.7 %copy-start.14 = (f32[128,4,1024]{0,2,1:T(8,128)S(1)}, f32[128,4,1024]{0,2,1:T(8,128)}, u32[]{:S(2)}) copy-start(f32[128,4,1024]{0,2,1:T(8,128)} %get-tuple-element.58) | copy-start | bytes 6291460
  239.5 5.6 %copy-start.12 = (bf16[128,4,1024]{0,2,1:T(8,128)(2,1)S(1)}, bf16[128,4,1024]{0,2,1:T(8,128)(2,1)}, u32[]{:S(2)}) copy-start(bf16[128,4,1024]{0,2,1:T(8,128)(2,1)} %copy-done.11) | copy-start | bytes 3145732
  241.8 3.4 copy-start.3
  245.1 1.8 copy-start.6
  249.4 3.1 copy-start.5
  249.4 3.1 copy-start.8
  274.7 18.8 %all-to-all-start.4 = ((bf16[4,128,1024]{2,1,0:T(8,128)(2,1)}), bf16[4,128,1024]{2,1,0:T(8,128)(2,1)}, u32[]{:S(2)}, u32[]{:S(2)}) async-start(bf16[4,128,1024]{2,1,0:T(8,128)(2,1)} %bitcast.41), calls=%async_computation.5 | async-start | bytes 2097152 | tf_op jit(solution)/shard_map/all_to_all | solution.py:184
  279.0 18.9 %copy-start.7 = (bf16[4,256,64,16]{1,3,0,2:T(8,128)(2,1)S(1)}, bf16[4,256,64,16]{1,3,0,2:T(8,128)(2,1)}, u32[]{:S(2)}) copy-start(bf16[4,256,64,16]{1,3,0,2:T(8,128)(2,1)} %copy-done.6) | copy-start | bytes 6291460
  279.0 18.9 %copy-start.10 = (bf16[4,128,64,16]{1,0,3,2:T(4,128)(2,1)S(1)}, bf16[4,128,64,16]{1,0,3,2:T(4,128)(2,1)}, u32[]{:S(2)}) copy-start(bf16[4,128,64,16]{1,0,3,2:T(4,128)(2,1)} %copy-done.9) | copy-start | bytes 3145732
  293.4 77.9 %all-to-all-start.5 = ((bf16[4,128,1024]{2,1,0:T(8,128)(2,1)}), bf16[4,128,1024]{2,1,0:T(8,128)(2,1)}, u32[]{:S(2)}, u32[]{:S(2)}) async-start(bf16[4,128,1024]{2,1,0:T(8,128)(2,1)} %bitcast.170), calls=%async_computation.6 | async-start | bytes 2097152 | tf_op jit(solution)/shard_map/all_to_all | solution.py:187
  322.2 44.9 %copy-start.16 = (bf16[4,128,1024]{2,1,0:T(8,128)(2,1)S(1)}, bf16[4,128,1024]{2,1,0:T(8,128)(2,1)}, u32[]{:S(2)}) copy-start(bf16[4,128,1024]{2,1,0:T(8,128)(2,1)} %all_to_all.108) | copy-start | bytes 3145732
  373.0 46.2 %copy-start.1 = (bf16[128,256]{1,0:T(8,128)(2,1)S(1)}, bf16[128,256]{1,0:T(8,128)(2,1)}, u32[]{:S(2)}) copy-start(bf16[128,256]{1,0:T(8,128)(2,1)} %param.12) | copy-start | bytes 196612
Sparse Core Ops, SparseCore 0:
  9.6 52.1 all-gather.2
  63.9 125.1 all-gather.4
  223.5 148.3 reduce-scatter.4
  375.1 44.0 reduce-scatter.2
where the time goes:
time: 431 us; the launch traced here: 426 us
  waiting for transfers between devices  168 us (39%)
  local copies, waits for them, and re-layouts  87.2 us (20%)
  blocking collectives  54.5 us (13%)
  other arithmetic  48.7 us (11%)
  matrix products  32.8 us (8%)
  starting transfers between devices  20.6 us (5%)
  between operations  14.4 us (3%)
    all_gather x1, waiting for transfers between devices, local(): weight_block = lax.all_gather(value_weight, 'dp', axis=0, tiled=True)  97.8 us
    reduce_scatter x1, waiting for transfers between devices, local(): lax.psum_scatter(lax.dot_general(grad_values, weight_block, (((1,), (1,))...  42.6 us
    psum x1, blocking collectives, local(): lax.psum((short_grad * row_scale).astype(jnp.bfloat16), 'dp')  36.9 us
    unnamed x55, local copies, waits for them, and re-layouts  23.5 us
    reduce_sum x3, other arithmetic, conv_taps_grad(): jnp.sum(gradient * extended[conv_edge - shift_back:conv_edge - shift_back...  20.1 us
    all_to_all x1, waiting for transfers between devices, local(): lax.all_to_all(gate_out, 'ctx', split_axis=1, concat_axis=0, tiled=True)  19.7 us
    all_to_all x1, blocking collectives, local(): lax.all_to_all(out_block, 'ctx', split_axis=0, concat_axis=1, tiled=True)  17.6 us
    reshape x1, local copies, waits for them, and re-layouts, fold_table(): flat.reshape(group_count, filter_span, double_span + 1)  14.3 us
  transfers between devices with their start and end apart: 9, of which 4 were waited for; matrix products, arithmetic and copies ran while one was open for 33% of the time, Pallas kernels for 0%

commit v1 on v0

--- a/solution.py
+++ b/solution.py
@@ -179,7 +179,28 @@
         jnp.zeros_like,
         zero_tuple,
     )
-    layer_out = lax.all_to_all(out_block, "ctx", split_axis=0, concat_axis=1, tiled=True)
+
+    def launch_sites_in(body, axis_tag):
+        wide_out = jax.lax.axis_size(axis_tag)
+        vec_out = jax.lax.axis_index(axis_tag)
+        x_now, found_now = (wide_out, vec_out)
+        shaped = body.shape[0] // x_now
+        base_arr = list(body.shape)
+        base_arr[0] = shaped
+        even = base_arr[1]
+        base_arr[1] = even * x_now
+        opened = jnp.zeros(base_arr, body.dtype)
+        for src_i in range(x_now):
+            w_next = lax.dynamic_slice_in_dim(body, (found_now ^ src_i) * shaped, shaped, axis=0)
+            if src_i:
+                main = tuple(((hop_no, hop_no ^ src_i) for hop_no in range(x_now)))
+                w_next = jax.lax.ppermute(w_next, axis_tag, main)
+            opened = lax.dynamic_update_slice_in_dim(
+                opened, w_next, (found_now ^ src_i) * even, axis=1
+            )
+        return opened
+
+    layer_out = launch_sites_in(out_block, "ctx")
     grad_gate_in, grad_gate_out = (
         lax.all_to_all(
             grad_streams[0].astype(jnp.bfloat16), "ctx", split_axis=0, concat_axis=1, tiled=True

time: 431 us -> 431 us (level)
  waiting for transfers between devices: 168 us -> 195 us
  blocking collectives: 54.5 us -> 35.2 us
  local copies, waits for them, and re-layouts: 87.2 us -> 80.1 us
    reduce_scatter x1, waiting for transfers between devices: 0.01 us -> 27.2 us  [local(): lax.psum_scatter((lax.dot_general(feature_window, grad_values, (((0,), (0...]
    all_to_all x1 -> x0, blocking collectives: 17.6 us -> none  [local(): lax.all_to_all(out_block, 'ctx', split_axis=0, concat_axis=1, tiled=True)]
    convert_element_type x1 -> x0, other arithmetic: 8.33 us -> none  [local(): grad_streams[1].astype(jnp.bfloat16)]
    all_to_all x1, waiting for transfers between devices: 6.1 us -> 0.01 us  [local(): lax.all_to_all(grad_streams[0].astype(jnp.bfloat16), 'ctx', split_axis=0,...]
    all_to_all x0 -> x1, other arithmetic: none -> 5.21 us  [local(): lax.all_to_all(grad_streams[1].astype(jnp.bfloat16), 'ctx', split_axis=0,...]
    unnamed x55 -> x66, local copies, waits for them, and re-layouts: 23.5 us -> 21.2 us
  transfers between devices with their start and end apart: 9 -> 12, of which waited for: 4 -> 5; matrix products, arithmetic and copies ran while one was open for 33% -> 30% of each run, Pallas kernels for 0% -> 0%
where the time goes in v1:
time: 431 us; the launch traced here: 425 us
  waiting for transfers between devices  195 us (45%)
  local copies, waits for them, and re-layouts  80.1 us (19%)
  other arithmetic  44.6 us (10%)
  blocking collectives  35.2 us (8%)
  matrix products  34.5 us (8%)
  starting transfers between devices  21.3 us (5%)
  between operations  14.6 us (3%)
    all_gather x1, waiting for transfers between devices, local(): weight_block = lax.all_gather(value_weight, 'dp', axis=0, tiled=True)  101 us
    reduce_scatter x1, waiting for transfers between devices, local(): lax.psum_scatter(lax.dot_general(grad_values, weight_block, (((1,), (1,))...  44.4 us
    psum x1, blocking collectives, local(): lax.psum((short_grad * row_scale).astype(jnp.bfloat16), 'dp')  35.2 us
    reduce_scatter x1, waiting for transfers between devices, local(): lax.psum_scatter((lax.dot_general(feature_window, grad_values, (((0,), (0...  27.2 us
    unnamed x66, local copies, waits for them, and re-layouts  21.2 us
    reduce_sum x3, other arithmetic, conv_taps_grad(): jnp.sum(gradient * extended[conv_edge - shift_back:conv_edge - shift_back...  20.4 us
    all_to_all x1, waiting for transfers between devices, local(): lax.all_to_all(gate_out, 'ctx', split_axis=1, concat_axis=0, tiled=True)  19.7 us
    reshape x1, local copies, waits for them, and re-layouts, fold_table(): flat.reshape(group_count, filter_span, double_span + 1)  14.2 us
  transfers between devices with their start and end apart: 12, of which 5 were waited for; matrix products, arithmetic and copies ran while one was open for 30% of the time, Pallas kernels for 0%

profile of v1, /device:TPU:0, one launch (start us, length us, event | category | flops | bytes accessed | tf_op | source)
XLA Modules:
  0.0 425.5 jit_solution(13932080816840971028)
XLA Ops:
  10.0 4.2 all-to-all-start
  15.5 19.7 %all-to-all-done = bf16[128,4,1024]{0,2,1:T(8,128)(2,1)S(1)} async-done(((bf16[128,4,1024]{0,2,1:T(8,128)(2,1)}), bf16[128,4,1024]{0,2,1:T(8,128)(2,1)S(1)}, u32[]{:S(2)}, u32[]{:S(2)}) %all-to-all-start) | async-done | bytes 1048608 | tf_op jit(solution)/shard_map/all_to_all | solution.py:164
  35.3 3.5 all-to-all-start.2
  39.3 3.2 tile.4
  42.5 10.9 %tile.10 = bf16[64,32896]{1,0:T(8,128)(2,1)} reshape(bf16[64,128,257]{2,1,0:T(8,128)(2,1)} %tile.4) | data formatting | bytes 8421376 | tf_op jit(solution)/shard_map/tile | solution.py:57
  53.3 2.2 slice-done
  55.5 3.2 copy.88
  63.4 3.5 all-to-all-start.1
  67.0 2.8 fusion.72
  69.8 4.8 %fusion.55 = (bf16[512,1024]{0,1:T(8,128)(2,1)S(1)}, f32[512,1024]{0,1:T(8,128)}) fusion(f32[4,128,8,128]{3,2,1,0:T(8,128)S(1)} %get-tuple-element.59, f32[1024]{0:T(1024)S(1)} %bitcast.195, f32[1024]{0:T(1024)S(1)} %bitcast.197, f32[1024]{0:T(1024)S(1)} %bitcast.199, f32[1024]{0:T(1024)S(1)} %bitcast.201, f32[1024]{0:T(1024)S(1)} %bitcast.203, ...), kind=kLoop, calls=%fused_computation.107 | loop fusion | flops 11534336 | bytes 6320128 | tf_op jit(solution)/shard_map/convert_element_type | solution.py:128
  75.8 2.6 concatenate.42
  79.7 2.4 fusion.56
  87.7 101.5 %all-gather.5.cloned.1.call-done = bf16[4096,1024]{1,0:T(8,128)(2,1)} async-done(((bf16[512,1024]{1,0:T(8,128)(2,1)}), bf16[4096,1024]{1,0:T(8,128)(2,1)}) %all-gather.5.cloned.1.call-update) | async-done | bytes 8388624 | tf_op jit(solution)/shard_map/all_gather | solution.py:157
  189.1 10.1 %convolution_convert_fusion.1 = bf16[512,1024]{1,0:T(8,128)(2,1)} fusion(bf16[512,4096]{1,0:T(8,128)(2,1)} %all-gather.3.cloned.1.call-done, bf16[4096,1024]{1,0:T(8,128)(2,1)} %all-gather.5.cloned.1.call-done), kind=kOutput, calls=%fused_computation.120 | convolution fusion | flops 4295491584 | bytes 13631488 | tf_op jit(solution)/shard_map/dot_general | solution.py:159
  199.3 8.6 %fusion.27 = (f32[1024]{0:T(1024)S(1)}, f32[1024]{0:T(1024)S(1)}, f32[1024]{0:T(1024)S(1)}, f32[1024]{0:T(1024)S(1)}, f32[1024]{0:T(1024)S(1)}, /*index=5*/f32[1...) fusion(bf16[512,1024]{1,0:T(8,128)(2,1)S(1)} %bitcast.167, ...), kind=kLoop, calls=%fused_computation.75 | loop fusion | flops 22012928 | bytes 9494528 | tf_op jit(solution)/shard_map/reduce_sum | solution.py:38
  207.9 6.5 %fusion.40 = (f32[1024]{0:T(1024)S(1)}, f32[1024]{0:T(1024)S(1)}, f32[1024]{0:T(1024)S(1)}, f32[1024]{0:T(1024)S(1)}, f32[1024]{0:T(1024)S(1)}, /*index=5*/f32[1...) fusion(bf16[512,1024]{1,0:T(8,128)(2,1)S(1)} %copy-done.16, ...), kind=kLoop, calls=%fused_computation.88 | loop fusion | flops 29352960 | bytes 11591680 | tf_op jit(solution)/shard_map/reduce_sum | solution.py:38
  216.2 7.0 %fusion = bf16[4096,1024]{0,1:T(8,128)(2,1)} fusion(bf16[512,1024]{1,0:T(8,128)(2,1)S(1)} %add_convert_fusion.1, bf16[512,4096]{1,0:T(8,128)(2,1)S(1)} %copy-done.28), kind=kOutput, calls=%fused_computation.1 | convolution fusion | flops 4303355904 | bytes 13631488 | tf_op jit(solution)/shard_map/dot_general | solution.py:219
  223.3 9.5 %convolution_convert_fusion = bf16[512,4096]{1,0:T(8,128)(2,1)} fusion(bf16[512,1024]{1,0:T(8,128)(2,1)S(1)} %add_convert_fusion.1, bf16[4096,1024]{1,0:T(8,128)(2,1)} %all-gather.5.cloned.1.call-done), kind=kOutput, calls=%fused_computation.2 | convolution fusion | flops 4297064448 | bytes 13631488 | tf_op jit(solution)/shard_map/dot_general | solution.py:232
  243.0 3.5 fusion.58
  248.5 5.2 %fusion.14 = (f32[1024]{0:T(1024)}, f32[1024]{0:T(1024)}, f32[1024]{0:T(1024)}, f32[1024]{0:T(1024)}, f32[1024]{0:T(1024)}, /*index=5*/f32[1024]{0:T(1024)}, f32[512,1024]{0,1:T(8,128)}, bf16[512,1024]{0,1:T(8,128)(2,1)S(1)}) fusion(bf16[512,1024]{0,1:T(8,128)(2,1)S(1)} %copy-done.7, f32[128,8,4,128]{3,2,1,0:T(4,128)S(1)} %bitcast.172, ...), kind=kLoop, calls=%fused_computation.62 | loop fusion | flops 11003904 | bytes 10510336 | tf_op jit(solution)/shard_map/reduce_sum | solution.py:38
  256.5 4.5 %all-to-all-start.3 = ((bf16[4,128,1024]{2,1,0:T(8,128)(2,1)}), bf16[4,128,1024]{2,1,0:T(8,128)(2,1)}, u32[]{:S(2)}, u32[]{:S(2)}) async-start(bf16[4,128,1024]{2,1,0:T(8,128)(2,1)} %bitcast.173), calls=%async_computation.4 | async-start | bytes 2097152 | tf_op jit(solution)/shard_map/all_to_all | solution.py:205
  262.3 4.7 %copy.92 = f32[8,8,128,256]{3,1,2,0:T(8,128)S(1)} copy(f32[8,8,128,256]{3,2,1,0:T(8,128)S(1)} %bitcast.165) | data formatting | bytes 16777216
  267.1 3.8 concatenate.46
  270.9 14.2 %reshape.120 = f32[64,128,257]{2,1,0:T(8,128)} reshape(f32[64,32896]{1,0:T(8,128)} %concatenate.46) | data formatting | bytes 16842752 | tf_op jit(solution)/shard_map/reshape | solution.py:67
  285.1 6.3 %reduce_sum.219 = f32[64,257]{1,0:T(8,128)S(1)} reduce(f32[64,128,257]{2,1,0:T(8,128)} %reshape.120, f32[]{:T(128)} %constant.5.clone.1), dimensions={1}, to_apply=%region_24.0 | reduce | flops 2088896 | bytes 8487172 | tf_op jit(solution)/shard_map/reduce_sum | solution.py:67
  291.6 5.2 %copy_bitcast_fusion.2 = bf16[4,128,1024]{1,2,0:T(8,128)(2,1)} fusion(f32[512,1024]{0,1:T(8,128)S(1)} %copy-done.14, f32[1024]{0:T(1024)S(1)} %bitcast.196, f32[1024]{0:T(1024)S(1)} %bitcast.198, f32[1024]{0:T(1024)S(1)} %bitcast.200, f32[1024]{0:T(1024)S(1)} %bitcast.202, f32[1024]{0:T(1024)S(1)} %bitcast.204, f32[1024]{0:T(1024)S(1)} %bitcast.206, ...), kind=kLoop, calls=%fused_computation.129 | loop fusion | flops 7340032 | bytes 3174400 | tf_op jit(solution)/shard_map/all_to_all | solution.py:208
  296.8 3.5 all-to-all-start.4
  300.9 35.2 %all-reduce.9 = (bf16[3,7,1024]{2,1,0:T(8,128)(2,1)S(1)}, bf16[128,64]{0,1:T(8,128)(2,1)S(1)}) all-reduce(bf16[3,7,1024]{2,1,0:T(8,128)(2,1)S(1)} %fusion.67, bf16[128,64]{0,1:T(8,128)(2,1)S(1)} %fusion.68), channel_id=1, replica_groups=mesh['dp'=8,'ctx'=4] {'dp'}, use_global_device_ids=true, to_apply=%region_23.0 | all-reduce | flops 29696 | bytes 118784 | tf_op jit(solution)/shard_map/psum | solution.py:214
  340.9 2.7 copy.87
  344.9 27.2 %reduce-scatter.5.cloned.1.call-done = bf16[512,1024]{0,1:T(8,128)(2,1)} async-done(((bf16[4096,1024]{0,1:T(8,128)(2,1)}), bf16[512,1024]{0,1:T(8,128)(2,1)}) %reduce-scatter.5.cloned.1.call-update) | async-done | bytes 1048592 | tf_op jit(solution)/shard_map/reduce_scatter | solution.py:217
  372.1 2.3 copy.78
  374.3 44.4 %reduce-scatter.3.cloned.1.call-done = bf16[128,4096]{1,0:T(8,128)(2,1)} async-done(((bf16[512,4096]{1,0:T(8,128)(2,1)}), bf16[128,4096]{1,0:T(8,128)(2,1)}) %reduce-scatter.3.cloned.1.call-update) | async-done | bytes 1048592 | tf_op jit(solution)/shard_map/reduce_scatter | solution.py:231
  (129 shorter events, 42.1 us)
Async XLA Ops:
  7.2 31.6 %copy-start = (bf16[128,256]{1,0:T(8,128)(2,1)S(1)}, bf16[128,256]{1,0:T(8,128)(2,1)}, u32[]{:S(2)}) copy-start(bf16[128,256]{1,0:T(8,128)(2,1)} %param.12) | copy-start | bytes 196612
  7.2 80.5 %all-gather.3.cloned.1.call-start = ((), (), s32[]{:S(2)}) async-start(), calls=%async_computation.7 | async-start | bytes 5242880 | tf_op jit(solution)/shard_map/all_gather | solution.py:158
  7.9 181.2 %all-gather.5.cloned.1.call-start = ((), (), s32[]{:S(2)}) async-start(), calls=%async_computation.8 | async-start | bytes 9437184 | tf_op jit(solution)/shard_map/all_gather | solution.py:157
  8.7 5.6 %copy-start.18 = (bf16[128,4096]{1,0:T(8,128)(2,1)S(1)}, bf16[128,4096]{1,0:T(8,128)(2,1)}, u32[]{:S(2)}) copy-start(bf16[128,4096]{1,0:T(8,128)(2,1)} %param.13) | copy-start | bytes 3145732
  10.0 25.3 %all-to-all-start = ((bf16[128,4,1024]{0,2,1:T(8,128)(2,1)}), bf16[128,4,1024]{0,2,1:T(8,128)(2,1)S(1)}, u32[]{:S(2)}, u32[]{:S(2)}) async-start(bf16[128,4,1024]{0,2,1:T(8,128)(2,1)} %bitcast.1), calls=%async_computation | async-start | bytes 2097152 | tf_op jit(solution)/shard_map/all_to_all | solution.py:164
  35.3 25.9 %copy-start.10 = (bf16[128,4,1024]{0,2,1:T(8,128)(2,1)}, bf16[128,4,1024]{0,2,1:T(8,128)(2,1)S(1)}, u32[]{:S(2)}) copy-start(bf16[128,4,1024]{0,2,1:T(8,128)(2,1)S(1)} %all-to-all-done) | copy-start | bytes 3145732
  35.3 27.1 %all-to-all-start.2 = ((bf16[128,4,1024]{0,2,1:T(8,128)(2,1)}), bf16[128,4,1024]{0,2,1:T(8,128)(2,1)S(1)}, u32[]{:S(2)}, u32[]{:S(2)}) async-start(bf16[128,4,1024]{0,2,1:T(8,128)(2,1)} %bitcast.29), calls=%async_computation.2 | async-start | bytes 2097152 | tf_op jit(solution)/shard_map/all_to_all | solution.py:165
  61.3 8.4 %copy-start.6 = (bf16[512,1024]{0,1:T(8,128)(2,1)}, bf16[512,1024]{0,1:T(8,128)(2,1)S(1)}, u32[]{:S(2)}) copy-start(bf16[512,1024]{0,1:T(8,128)(2,1)S(1)} %copy_bitcast_fusion.1) | copy-start | bytes 3145732
  63.4 135.9 %all-to-all-start.1 = ((bf16[128,4,1024]{2,0,1:T(8,128)(2,1)}), bf16[128,4,1024]{2,0,1:T(8,128)(2,1)S(1)}, u32[]{:S(2)}, u32[]{:S(2)}) async-start(bf16[128,4,1024]{2,0,1:T(8,128)(2,1)} %bitcast.175), calls=%async_computation.1 | async-start | bytes 2097152 | tf_op jit(solution)/shard_map/all_to_all | solution.py:163
  66.9 305.2 %reduce-scatter.5.cloned.1.call-start = ((), (), s32[]{:S(2)}) async-start(), calls=%async_computation.10 | async-start | bytes 9437184 | tf_op jit(solution)/shard_map/reduce_scatter | solution.py:217
  69.7 4.8 %copy-start.4 = (f32[4,128,8,128]{3,2,1,0:T(8,128)}, f32[4,128,8,128]{3,2,1,0:T(8,128)S(1)}, u32[]{:S(2)}) copy-start(f32[4,128,8,128]{3,2,1,0:T(8,128)S(1)} %get-tuple-element.59) | copy-start | bytes 6291460
  75.8 6.4 %copy-start.8 = (bf16[4,128,64,16]{1,0,3,2:T(4,128)(2,1)}, bf16[4,128,64,16]{1,0,3,2:T(4,128)(2,1)S(1)}, u32[]{:S(2)}) copy-start(bf16[4,128,64,16]{1,0,3,2:T(4,128)(2,1)S(1)} %reshape.116) | copy-start | bytes 3145732
  199.3 8.7 %copy-start.16 = (bf16[512,1024]{1,0:T(8,128)(2,1)S(1)}, bf16[512,1024]{1,0:T(8,128)(2,1)}, u32[]{:S(2)}) copy-start(bf16[512,1024]{1,0:T(8,128)(2,1)} %convolution_convert_fusion.1) | copy-start | bytes 3145732
  207.9 8.3 %copy-start.28 = (bf16[512,4096]{1,0:T(8,128)(2,1)S(1)}, bf16[512,4096]{1,0:T(8,128)(2,1)}, u32[]{:S(2)}) copy-start(bf16[512,4096]{1,0:T(8,128)(2,1)} %all-gather.3.cloned.1.call-done) | copy-start | bytes 12582916
  223.3 195.4 %reduce-scatter.3.cloned.1.call-start = ((), (), s32[]{:S(2)}) async-start(), calls=%async_computation.9 | async-start | bytes 5242880 | tf_op jit(solution)/shard_map/reduce_scatter | solution.py:231
  238.6 4.4 %copy-start.11 = (bf16[128,4,1024]{0,2,1:T(8,128)(2,1)S(1)}, bf16[128,4,1024]{0,2,1:T(8,128)(2,1)}, u32[]{:S(2)}) copy-start(bf16[128,4,1024]{0,2,1:T(8,128)(2,1)} %copy-done.10) | copy-start | bytes 3145732
  243.0 4.5 %copy-start.13 = (f32[512,1024]{0,1:T(8,128)S(1)}, f32[512,1024]{0,1:T(8,128)}, u32[]{:S(2)}) copy-start(f32[512,1024]{0,1:T(8,128)} %get-tuple-element.56) | copy-start | bytes 6291460
  253.7 7.3 %copy-start.9 = (bf16[4,128,64,16]{1,0,3,2:T(4,128)(2,1)S(1)}, bf16[4,128,64,16]{1,0,3,2:T(4,128)(2,1)}, u32[]{:S(2)}) copy-start(bf16[4,128,64,16]{1,0,3,2:T(4,128)(2,1)} %copy-done.8) | copy-start | bytes 3145732
  254.7 82.8 %collective-permute-start = (bf16[128,1024]{0,1:T(8,128)(2,1)}, bf16[128,1024]{0,1:T(8,128)(2,1)}, u32[]{:S(2)}, u32[]{:S(2)}) collective-permute-start(bf16[128,1024]{0,1:T(8,128)(2,1)} %get-tuple-element.62), channel_id=1, source_target_pairs={{0,1},{1,0},{2,3},{3,2},{4,5},{5,4},{6,7},{7,6},{8,9},{9,8},{10,11... | collective-permute-start | bytes 786440 | tf_op jit(solution)/shard_map/ppermute | solution.py:197
  254.7 83.9 %collective-permute-start.1 = (bf16[128,1024]{0,1:T(8,128)(2,1)}, bf16[128,1024]{0,1:T(8,128)(2,1)}, u32[]{:S(2)}, u32[]{:S(2)}) collective-permute-start(bf16[128,1024]{0,1:T(8,128)(2,1)} %get-tuple-element.61), channel_id=1, source_target_pairs={{0,2},{1,3},{2,0},{3,1},{4,6},{5,7},{6,4},{7,5},{8,10},{9,11},{10,... | collective-permute-start | bytes 786440 | tf_op jit(solution)/shard_map/ppermute | solution.py:197
  256.2 83.5 %collective-permute-start.2 = (bf16[128,1024]{0,1:T(8,128)(2,1)}, bf16[128,1024]{0,1:T(8,128)(2,1)}, u32[]{:S(2)}, u32[]{:S(2)}) collective-permute-start(bf16[128,1024]{0,1:T(8,128)(2,1)} %get-tuple-element.60), channel_id=1, source_target_pairs={{0,3},{1,2},{2,1},{3,0},{4,7},{5,6},{6,5},{7,4},{8,11},{9,10},{10,... | collective-permute-start | bytes 786440 | tf_op jit(solution)/shard_map/ppermute | solution.py:197
  256.5 40.3 %all-to-all-start.3 = ((bf16[4,128,1024]{2,1,0:T(8,128)(2,1)}), bf16[4,128,1024]{2,1,0:T(8,128)(2,1)}, u32[]{:S(2)}, u32[]{:S(2)}) async-start(bf16[4,128,1024]{2,1,0:T(8,128)(2,1)} %bitcast.173), calls=%async_computation.4 | async-start | bytes 2097152 | tf_op jit(solution)/shard_map/all_to_all | solution.py:205
  285.1 6.5 %copy-start.14 = (f32[512,1024]{0,1:T(8,128)S(1)}, f32[512,1024]{0,1:T(8,128)}, u32[]{:S(2)}) copy-start(f32[512,1024]{0,1:T(8,128)} %get-tuple-element.52) | copy-start | bytes 6291460
  296.8 3.9 copy-start.23
  296.8 3.9 copy-start.24
  296.8 3.9 copy-start.25
  296.8 3.9 copy-start.26
  296.8 3.9 copy-start.27
  296.8 4.0 copy-start.21
  296.8 46.7 %all-to-all-start.4 = ((bf16[4,128,1024]{1,2,0:T(8,128)(2,1)}), bf16[4,128,1024]{1,2,0:T(8,128)(2,1)S(1)}, u32[]{:S(2)}, u32[]{:S(2)}) async-start(bf16[4,128,1024]{1,2,0:T(8,128)(2,1)} %copy_bitcast_fusion.2), calls=%async_computation.5 | async-start | bytes 2097152 | tf_op jit(solution)/shard_map/all_to_all | solution.py:208
  340.9 4.0 copy-start.20
  343.6 75.1 %copy-start.1 = (bf16[128,256]{1,0:T(8,128)(2,1)S(1)}, bf16[128,256]{1,0:T(8,128)(2,1)}, u32[]{:S(2)}) copy-start(bf16[128,256]{1,0:T(8,128)(2,1)} %param.12) | copy-start | bytes 196612
  (10 other events, 23.1 us)
Sparse Core Ops, SparseCore 0:
  9.6 52.1 all-gather.2
  63.9 125.1 all-gather.4
  223.4 148.6 reduce-scatter.4
  375.2 43.4 reduce-scatter.2
